TPU v7x, 256 devices: a whole 4x4x8 slice. The times are simulated.
256 devices in a mesh: blk: 32 (over x, z), leaf: 4 (over y), samp: 2 (over core).
Axes of the slice: x: 4, y: 4, z: 8, core: 2. Of those that a mesh axis runs over, the one named last changes fastest.
Arguments:
- points: float32 [3, 32768], P(None, ('blk', 'leaf')), may hold values from 0 to 64, as said below
- neighbors: int32 [128, 8], P(('blk', 'leaf')), may hold values from -1 to 127, as said below
- omega: float32 [512, 32768], P(None, ('blk', 'leaf')), may hold values from -6 to 6
- observed: float32 [32768], P(('blk', 'leaf')), may hold values from -6 to 6
- prior_draws: float32 [64, 32768], P('samp', ('blk', 'leaf')), may hold values from -6 to 6
Outputs:
- weights: float32 [64, 32768], P('samp', ('blk', 'leaf'))
- residual: float32 [64, 32768], P('samp', ('blk', 'leaf'))
Inputs may be any that keep to these rules, and one draw needn't show every extreme that they name: Block g's points lie in the unit cell with integer corner (cx, cy, cz), where cx // 2 = g // 4 and 0 <= cy, cz < 3. `neighbors`: row g lists in ascending order every block h whose unit cell touches g's (cells at most one apart in every coordinate, the first taken periodic of period 2 * 32), which includes every block with a point within distance 1 of a point of g, followed by -1 in the unused slots; the relation is symmetric, and every listed block has a slab index h // 4 equal to or cyclically next to g // 4.
All inputs are finite; a program needn't handle non-finite values.
Results may differ from a plain program's by a relative error of at most 0.0003.
Values sent between devices are 32-bit elements; how exact they have to be, the bound alone decides.
A program may use at most 64 MiB of HBM per device.

v0:
```python
import jax
import jax.numpy as jnp
from jax import lax
from jax.sharding import PartitionSpec as P

PB = 256
ITERS = 2
support_radius = 0.8
noise_variance = 1.0
sketch_shift = 1.0
ALL_AXES = ("blk", "leaf", "samp")


def shifted_2(block, axis, distance):
    devices = range(lax.axis_size(axis))
    route = [((i - distance) % len(devices), i) for i in devices]
    return lax.ppermute(block, axis, route)


def wendland(row_points, column_points, period):
    offset = row_points[None, :, :, None] - column_points[:, :, None, :]
    half_period = 0.5 * period
    along_x = jnp.mod(offset[:, 0] + half_period, period) - half_period
    squared = along_x * along_x + offset[:, 1] * offset[:, 1] + offset[:, 2] * offset[:, 2]
    radius = jnp.sqrt(squared) / support_radius
    remain = jnp.maximum(1.0 - radius, 0.0)
    return remain**4 * (4.0 * radius + 1.0)


def high_dot(left, right):
    return jnp.dot(left, right, precision=lax.Precision.HIGHEST, preferred_element_type=jnp.float32)


def shifted(values, offset_by):
    return shifted_2(values, "blk", offset_by)


def beside_all(values):
    slab_values = lax.all_gather(values, "leaf", axis=1, tiled=True)
    return jnp.concatenate([shifted(slab_values, 1), slab_values, shifted(slab_values, -1)], axis=1)


def lower_solve(factor, values):
    return lax.linalg.triangular_solve(factor, values, left_side=True, lower=True)


def local(points, neighbors, omega, observed, prior_draws):
    blk_dev = neighbors.shape[0]
    cycle_count = lax.axis_size("blk")
    slab_blocks = blk_dev * lax.axis_size("leaf")
    period = 2.0 * cycle_count
    own_slab = lax.axis_index("blk")
    n_samp = lax.axis_size("samp")
    samp_idx = lax.axis_index("samp")
    usable = neighbors >= 0
    relative = jnp.mod(neighbors // slab_blocks - own_slab + 1, cycle_count)
    chosen = jnp.where(usable, relative * slab_blocks + jnp.mod(neighbors, slab_blocks), 0)
    usable_weight = usable.astype(jnp.float32)
    reach_points = beside_all(points)
    reach_blocks = reach_points.reshape(3, 3 * slab_blocks, PB).transpose(1, 0, 2)
    row_blocks = points.reshape(3, blk_dev, PB).transpose(1, 0, 2)
    kernel_tile = wendland(row_blocks[0], reach_blocks[chosen[0]], period)
    kernel_tile = kernel_tile * usable_weight[0][:, None, None]

    def apply_kernel(values):
        width = values.shape[0]
        reach = beside_all(values).reshape(width, 3 * slab_blocks, PB)
        picked = jnp.take(reach, chosen[0], axis=1)
        return jnp.einsum("cnj,nij->ci", picked, kernel_tile, precision=lax.Precision.HIGHEST)

    def slot(x):
        zeros = jnp.zeros((n_samp,) + x.shape, x.dtype)
        return lax.dynamic_update_index_in_dim(zeros, x, samp_idx, 0)

    def unslot(xs):
        return lax.dynamic_index_in_dim(xs, samp_idx, 0, keepdims=False)

    def total_per_samp(values):
        return jax.tree.map(unslot, lax.psum(jax.tree.map(slot, values), ALL_AXES))

    sketch = apply_kernel(omega) + sketch_shift * omega
    rhs = observed[None, :] - prior_draws
    half = PB // n_samp
    omega_half = lax.dynamic_slice_in_dim(omega, samp_idx * half, half, axis=1)
    sketch_half = lax.dynamic_slice_in_dim(sketch, samp_idx * half, half, axis=1)
    core_part = high_dot(omega_half, sketch_half.T)
    square_part = high_dot(sketch_half, sketch_half.T)
    joint_part = 0.5 * (core_part + core_part.T) + 0.5 * (square_part + square_part.T)
    rhs_part = slot(high_dot(sketch, rhs.T))
    joint_gram, rhs_proj = lax.psum((joint_part, rhs_part), ALL_AXES)
    rhs_proj = unslot(rhs_proj)
    joint_factor = jnp.linalg.cholesky(joint_gram)

    def precond_from(vectors, projected):
        first_solve = lower_solve(joint_factor, projected)
        solved = lax.linalg.triangular_solve(
            joint_factor, first_solve, left_side=True, lower=True, transpose_a=True
        )
        return (vectors - high_dot(solved.T, sketch)) / noise_variance

    residual = rhs
    projected = rhs_proj
    precond = precond_from(residual, projected)
    direction = precond
    weights = jnp.zeros_like(rhs)
    image = apply_kernel(direction) + noise_variance * direction
    inner_now, curvature, image_proj = total_per_samp(
        (
            jnp.sum(residual * precond, axis=1),
            jnp.sum(direction * image, axis=1),
            high_dot(sketch, image.T),
        )
    )
    step_size = inner_now / curvature
    weights = weights + step_size[:, None] * direction
    residual = residual - step_size[:, None] * image
    projected = projected - step_size[None, :] * image_proj
    precond = precond_from(residual, projected)
    inner_next = total_per_samp(jnp.sum(residual * precond, axis=1))
    direction = precond + (inner_next / inner_now)[:, None] * direction
    inner_now = inner_next
    image = apply_kernel(direction) + noise_variance * direction
    curvature = total_per_samp(jnp.sum(direction * image, axis=1))
    step_size = inner_now / curvature
    weights = weights + step_size[:, None] * direction
    residual = residual - step_size[:, None] * image
    return (weights, residual)


def solution(mesh):
    in_specs = (
        P(None, ("blk", "leaf")),
        P(("blk", "leaf"), None),
        P(None, ("blk", "leaf")),
        P(("blk", "leaf")),
        P("samp", ("blk", "leaf")),
    )
    out_specs = (P("samp", ("blk", "leaf")), P("samp", ("blk", "leaf")))
    return jax.shard_map(local, mesh=mesh, in_specs=in_specs, out_specs=out_specs, check_vma=False)
```

profile of v0, /device:TPU:1, one launch (start us, length us, event | category | flops | bytes accessed | tf_op | source)
XLA Modules:
  0.0 1005.4 jit_solution(9335899095662480256)
XLA Ops:
  9.3 10.5 %all_gather.13 = f32[3,1024]{1,0:T(4,128)S(1)} all-gather(f32[3,256]{1,0:T(4,128)} %param.11), channel_id=1, replica_groups=mesh['blk'=32,'leaf'=4,'samp'=2] {'leaf'}, dimensions={1}, use_global_device_ids=true | all-gather | bytes 15360 | tf_op jit(solution)/shard_map/all_gather | solution.py:39
  19.9 7.8 collective-permute-start.3
  27.6 19.4 %all-gather.2.cloned.1.call-done = f32[512,1024]{0,1:T(8,128)} async-done(((f32[512,256]{0,1:T(8,128)}), f32[512,1024]{0,1:T(8,128)}) %all-gather.2.cloned.1.call-update) | async-done | bytes 2097168 | tf_op jit(solution)/shard_map/all_gather | solution.py:39
  58.3 38.5 %collective-permute-done.1 = f32[512,1024]{0,1:T(8,128)} collective-permute-done((f32[512,1024]{0,1:T(8,128)}, f32[512,1024]{0,1:T(8,128)}, u32[]{:S(2)}, u32[]{:S(2)}) %collective-permute-start.1) | collective-permute-done | bytes 2097184 | tf_op jit(solution)/shard_map/ppermute | solution.py:17
  102.2 5.6 pad_maximum_fusion
  107.8 6.5 copy.11
  114.3 5.6 gather_fusion
  119.9 5.5 fusion.17
  139.7 250.3 %all-reduce.8.cloned.1.call-done = (f32[512,512]{1,0:T(8,128)}, f32[2,512,32]{1,2,0:T(8,128)}) async-done(((f32[512,512]{1,0:T(8,128)}, f32[2,512,32]{1,2,0:T(8,128)}), (f32[512,512]{1,0:T(8,128)}, f32[2,512,32]{1,2,0:T(8,128)})) %all-reduce.8.cloned.1.call-update) | async-done | bytes 1179664 | tf_op jit(solution)/shard_map/psum | solution.py:90
  396.2 11.7 %cholesky.104 = f32[128,128]{1,0:T(8,128)S(1)} custom-call(f32[128,128]{1,0:T(8,128)S(1)} %cholesky.266), custom_call_target="Cholesky" | custom-call | tf_op jit(solution)/shard_map/jit(cholesky)/cholesky | solution.py:92
  407.9 9.8 custom-call.33
  422.1 11.7 %cholesky.217 = f32[128,128]{1,0:T(8,128)S(1)} custom-call(f32[128,128]{1,0:T(8,128)S(1)} %cholesky.270), custom_call_target="Cholesky" | custom-call | tf_op jit(solution)/shard_map/jit(cholesky)/cholesky | solution.py:92
  434.5 10.2 %custom-call.34 = f32[1,128,128]{1,2,0:T(8,128)S(1)} custom-call(f32[1,128,128]{2,1,0:T(8,128)S(1)} %get-tuple-element.61), custom_call_target="InvertDiagBlocksLowerTriangular" | custom-call | tf_op jit(solution)/shard_map/jit(cholesky)/cholesky | solution.py:92
  447.1 11.7 %cholesky.238 = f32[128,128]{1,0:T(8,128)S(1)} custom-call(f32[128,128]{1,0:T(8,128)S(1)} %cholesky.275), custom_call_target="Cholesky" | custom-call | tf_op jit(solution)/shard_map/jit(cholesky)/cholesky | solution.py:92
  460.2 9.8 custom-call.35
  472.3 11.7 %cholesky.255 = f32[128,128]{1,0:T(8,128)S(1)} custom-call(f32[128,128]{1,0:T(8,128)S(1)} %convolution_subtract_fusion.2), custom_call_target="Cholesky" | custom-call | tf_op jit(solution)/shard_map/jit(cholesky)/cholesky | solution.py:92
  491.1 12.0 %while.8 = (s32[]{:T(128)}, f32[512,512]{1,0:T(8,128)}, s32[4,2]{0,1:T(2,128)S(1)}, f32[4,128,128]{2,1,0:T(8,128)S(1)}, s32[]{:T(128)}) while((s32[]{:T(128)}, f32[512,512]{1,0:T(8,128)}, s32[4,2]{0,1:T(2,128)S(1)}, f32[4,128,128]{2,1,0:T(8,128)S(1)}, s32[]{:T(128)}) %tuple.51), condition=%wide.while_cond.1, body=%wide.while_body.1.sunk | while | flops 2 | bytes 131189 | solution.py:96
  503.1 39.3 %custom-call.39 = f32[4,128,128]{1,2,0:T(8,128)S(1)} custom-call(f32[4,128,128]{2,1,0:T(8,128)S(1)} %get-tuple-element.34), custom_call_target="InvertDiagBlocksLowerTriangular" | custom-call | tf_op jit(solution)/shard_map/triangular_solve/custom-call.8 | solution.py:96
  551.2 9.2 all_gather.14
  577.5 76.1 %all-reduce.1 = (f32[2,32]{1,0:T(2,128)S(1)}, f32[2,32]{1,0:T(2,128)S(1)}) all-reduce(f32[2,32]{1,0:T(2,128)S(1)} %dynamic_update_slice.22, f32[2,32]{1,0:T(2,128)S(1)} %dynamic_update_slice.21), channel_id=1, replica_groups=mesh['blk'=32,'leaf'=4,'samp'=2] {'blk','leaf','samp'}, use_global_device_ids=true, to_apply=%region_13.17 | all-reduce | flops 128 | bytes 1024 | tf_op jit(solution)/shard_map/psum | solution.py:79
  653.7 161.9 %all-reduce.6.cloned.1.call-done = f32[2,512,32]{1,2,0:T(8,128)} async-done(((f32[2,512,32]{1,2,0:T(8,128)}), f32[2,512,32]{1,2,0:T(8,128)}) %all-reduce.6.cloned.1.call-update) | async-done | bytes 131088 | tf_op jit(solution)/shard_map/psum | solution.py:79
  825.4 75.9 %psum.54 = f32[2,32]{1,0:T(2,128)S(1)} all-reduce(f32[2,32]{1,0:T(2,128)S(1)} %dynamic_update_slice.24), channel_id=1, replica_groups=mesh['blk'=32,'leaf'=4,'samp'=2] {'blk','leaf','samp'}, use_global_device_ids=true, to_apply=%region_16.20 | all-reduce | flops 64 | bytes 512 | tf_op jit(solution)/shard_map/psum | solution.py:79
  901.4 9.1 all_gather.15
  921.8 76.2 %psum.55 = f32[2,32]{1,0:T(2,128)S(1)} all-reduce(f32[2,32]{1,0:T(2,128)S(1)} %dynamic_update_slice.25), channel_id=1, replica_groups=mesh['blk'=32,'leaf'=4,'samp'=2] {'blk','leaf','samp'}, use_global_device_ids=true, to_apply=%region_18.22 | all-reduce | flops 64 | bytes 512 | tf_op jit(solution)/shard_map/psum | solution.py:79
  (152 shorter events, 114.0 us)
Async XLA Ops:
  7.2 39.9 %all-gather.2.cloned.1.call-start = ((), (), s32[]{:S(2)}) async-start(), calls=%async_computation | async-start | bytes 2621440 | tf_op jit(solution)/shard_map/all_gather | solution.py:39
  9.3 380.7 %all-reduce.8.cloned.1.call-start = ((), (), s32[]{:S(2)}) async-start(), calls=%async_computation.2 | async-start | bytes 2359296 | tf_op jit(solution)/shard_map/psum | solution.py:90
  19.9 33.9 %collective-permute-start.3 = (f32[3,1024]{1,0:T(4,128)S(1)}, f32[3,1024]{1,0:T(4,128)S(1)}, u32[]{:S(2)}, u32[]{:S(2)}) collective-permute-start(f32[3,1024]{1,0:T(4,128)S(1)} %all_gather.13), channel_id=1, source_target_pairs={{8,0},{16,8},{24,16},{32,24},{40,32},{48,40},{56,48},{64,56},{72,6... | collective-permute-start | bytes 36872 | tf_op jit(solution)/shard_map/ppermute | solution.py:17
  27.6 26.1 %collective-permute-start.2 = (f32[3,1024]{1,0:T(4,128)S(1)}, f32[3,1024]{1,0:T(4,128)S(1)}, u32[]{:S(2)}, u32[]{:S(2)}) collective-permute-start(f32[3,1024]{1,0:T(4,128)S(1)} %all_gather.13), channel_id=1, source_target_pairs={{248,0},{0,8},{8,16},{16,24},{24,32},{32,40},{40,48},{48,56},{56,6... | collective-permute-start | bytes 36872 | tf_op jit(solution)/shard_map/ppermute | solution.py:17
  47.1 49.8 %collective-permute-start.1 = (f32[512,1024]{0,1:T(8,128)}, f32[512,1024]{0,1:T(8,128)}, u32[]{:S(2)}, u32[]{:S(2)}) collective-permute-start(f32[512,1024]{0,1:T(8,128)} %all-gather.2.cloned.1.call-done), channel_id=1, source_target_pairs={{8,0},{16,8},{24,16},{32,24},{40,32},{48,40},{56,48},{64,56},{72,6... | collective-permute-start | bytes 6291464 | tf_op jit(solution)/shard_map/ppermute | solution.py:17
  52.2 50.0 %collective-permute-start = (f32[512,1024]{0,1:T(8,128)}, f32[512,1024]{0,1:T(8,128)}, u32[]{:S(2)}, u32[]{:S(2)}) collective-permute-start(f32[512,1024]{0,1:T(8,128)} %all-gather.2.cloned.1.call-done), channel_id=1, source_target_pairs={{248,0},{0,8},{8,16},{16,24},{24,32},{32,40},{40,48},{48,56},{56,6... | collective-permute-start | bytes 6291464 | tf_op jit(solution)/shard_map/ppermute | solution.py:17
  55.7 46.5 %copy-start.2 = (f32[512,1024]{0,1:T(8,128)S(1)}, f32[512,1024]{0,1:T(8,128)}, u32[]{:S(2)}) copy-start(f32[512,1024]{0,1:T(8,128)} %all-gather.2.cloned.1.call-done) | copy-start | bytes 6291460
  114.3 5.6 copy-start
  134.5 3.7 copy-start.5
  134.5 3.7 copy-start.10
  138.8 0.6 copy-start.7
  139.4 676.2 %all-reduce.6.cloned.1.call-start = ((), (), s32[]{:S(2)}) async-start(), calls=%async_computation.1 | async-start | bytes 262144 | tf_op jit(solution)/shard_map/psum | solution.py:79
  395.2 1.0 copy-start.1
  551.2 16.2 %copy-start.3 = (f32[32,256]{1,0:T(8,128)}, f32[32,256]{1,0:T(8,128)S(1)}, u32[]{:S(2)}) copy-start(f32[32,256]{1,0:T(8,128)S(1)} %convolution_subtract_fusion.4) | copy-start | bytes 98308
  560.4 7.0 collective-permute-start.5
  565.4 7.1 collective-permute-start.4
  573.2 80.4 %copy-start.6 = (f32[32,256]{1,0:T(8,128)S(1)}, f32[32,256]{1,0:T(8,128)}, u32[]{:S(2)}) copy-start(f32[32,256]{1,0:T(8,128)} %param.15) | copy-start | bytes 98308
  573.2 242.4 %copy-start.9 = (f32[2,512,32]{1,2,0:T(8,128)S(1)}, f32[2,512,32]{1,2,0:T(8,128)}, u32[]{:S(2)}) copy-start(f32[2,512,32]{1,2,0:T(8,128)} %get-tuple-element.50) | copy-start | bytes 393220
  576.1 325.3 %copy-start.4 = (f32[32,256]{1,0:T(8,128)S(1)}, f32[32,256]{1,0:T(8,128)}, u32[]{:S(2)}) copy-start(f32[32,256]{1,0:T(8,128)} %copy-done.3) | copy-start | bytes 98308
  576.7 0.7 copy-start.8
  910.5 4.0 collective-permute-start.7
  911.9 7.1 collective-permute-start.6
Sparse Core Ops, SparseCore 0:
  9.8 37.2 all-gather.1
  139.5 250.3 all-reduce.7
  577.5 238.0 all-reduce.5
where the time goes:
time: 1010 us
  waiting for transfers between devices  490 us (49%)
  blocking collectives  257 us (25%)
  other arithmetic  141 us (14%)
  matrix products  40.6 us (4%)
  local copies, waits for them, and re-layouts  40.1 us (4%)
  starting transfers between devices  20.1 us (2%)
  between operations  17.2 us (2%)
    psum x1, waiting for transfers between devices, local(): joint_gram, rhs_proj = lax.psum((joint_part, rhs_part), ALL_AXES)  250 us
    psum x3, blocking collectives, total_per_samp(): return jax.tree.map(unslot, lax.psum(jax.tree.map(slot, values), ALL_AXES))  228 us
    psum x1, waiting for transfers between devices, total_per_samp(): return jax.tree.map(unslot, lax.psum(jax.tree.map(slot, values), ALL_AXES))  162 us
    another operation x14, other arithmetic, local(): joint_factor = jnp.linalg.cholesky(joint_gram)  80.7 us
    ppermute x8, waiting for transfers between devices, shifted_2(): return lax.ppermute(block, axis, route)  57.9 us
    another operation x4, other arithmetic, precond_from(): lax.linalg.triangular_solve(joint_factor, first_solve, left_side=True, lo...  41.8 us
    all_gather x3, blocking collectives, beside_all(): slab_values = lax.all_gather(values, 'leaf', axis=1, tiled=True)  28.8 us
  transfers between devices with their start and end apart: 11, of which 9 were waited for; matrix products, arithmetic and copies ran while one was open for 1% of the time, Pallas kernels for 0%

commit v1 on v0

--- a/solution.py
+++ b/solution.py
@@ -36,7 +36,8 @@
 
 
 def beside_all(values):
-    slab_values = lax.all_gather(values, "leaf", axis=1, tiled=True)
+    copies = jnp.concatenate([values] * lax.axis_size("leaf"), axis=1)
+    slab_values = lax.all_to_all(copies, "leaf", 1, 1, tiled=True)
     return jnp.concatenate([shifted(slab_values, 1), slab_values, shifted(slab_values, -1)], axis=1)
 
 

time: 1010 us -> 1010 us (level)
  waiting for transfers between devices: 490 us -> 465 us
  blocking collectives: 257 us -> 270 us
    all_to_all x0 -> x3, blocking collectives: none -> 45.5 us  [beside_all(): slab_values = lax.all_to_all(copies, 'leaf', 1, 1, tiled=True)]
    all_gather x3 -> x0, blocking collectives: 28.8 us -> none  [beside_all(): slab_values = lax.all_gather(values, 'leaf', axis=1, tiled=True)]
    all_gather x1 -> x0, waiting for transfers between devices: 19.4 us -> none  [beside_all(): slab_values = lax.all_gather(values, 'leaf', axis=1, tiled=True)]
where the time goes in v1:
time: 1010 us; the launch traced here: 1000 us
  waiting for transfers between devices  465 us (46%)
  blocking collectives  270 us (27%)
  other arithmetic  140 us (14%)
  local copies, waits for them, and re-layouts  42.7 us (4%)
  matrix products  40.6 us (4%)
  starting transfers between devices  24.7 us (2%)
  between operations  17.6 us (2%)
    psum x1, waiting for transfers between devices, local(): joint_gram, rhs_proj = lax.psum((joint_part, rhs_part), ALL_AXES)  250 us
    psum x3, blocking collectives, total_per_samp(): return jax.tree.map(unslot, lax.psum(jax.tree.map(slot, values), ALL_AXES))  224 us
    psum x1, waiting for transfers between devices, total_per_samp(): return jax.tree.map(unslot, lax.psum(jax.tree.map(slot, values), ALL_AXES))  161 us
    another operation x14, other arithmetic, local(): joint_factor = jnp.linalg.cholesky(joint_gram)  80.7 us
    ppermute x8, waiting for transfers between devices, shifted_2(): return lax.ppermute(block, axis, route)  49.6 us
    all_to_all x3, blocking collectives, beside_all(): slab_values = lax.all_to_all(copies, 'leaf', 1, 1, tiled=True)  45.5 us
    another operation x4, other arithmetic, precond_from(): lax.linalg.triangular_solve(joint_factor, first_solve, left_side=True, lo...  41.8 us
    ppermute x8, starting transfers between devices, shifted_2(): return lax.ppermute(block, axis, route)  21.1 us
  transfers between devices with their start and end apart: 11, of which 9 were waited for; matrix products, arithmetic and copies ran while one was open for 1% of the time, Pallas kernels for 0%

profile of v1, /device:TPU:1, one launch (start us, length us, event | category | flops | bytes accessed | tf_op | source)
XLA Modules:
  0.0 1000.5 jit_solution(16555393048090665377)
XLA Ops:
  10.6 29.6 %all_to_all.48 = f32[512,4,256]{2,0,1:T(8,128)S(1)} all-to-all(f32[512,4,256]{2,0,1:T(8,128)} %copy.20), channel_id=1, replica_groups=mesh['blk'=32,'leaf'=4,'samp'=2] {'leaf'}, dimensions={1} | all-to-all | bytes 4194304 | tf_op jit(solution)/shard_map/all_to_all | solution.py:40
  42.2 8.6 collective-permute-start.1
  64.2 30.2 %collective-permute-done.3 = f32[3,1024]{1,0:T(4,128)S(1)} collective-permute-done((f32[3,1024]{1,0:T(4,128)S(1)}, f32[3,1024]{1,0:T(4,128)S(1)}, u32[]{:S(2)}, u32[]{:S(2)}) %collective-permute-start.3) | collective-permute-done | bytes 12320 | tf_op jit(solution)/shard_map/ppermute | solution.py:17
  94.4 5.3 collective-permute-done.2
  109.5 5.9 pad_maximum_fusion
  115.4 5.7 gather_fusion
  121.1 5.5 fusion.17
  140.9 250.4 %all-reduce.8.cloned.1.call-done = (f32[512,512]{1,0:T(8,128)}, f32[2,512,32]{1,2,0:T(8,128)}) async-done(((f32[512,512]{1,0:T(8,128)}, f32[2,512,32]{1,2,0:T(8,128)}), (f32[512,512]{1,0:T(8,128)}, f32[2,512,32]{1,2,0:T(8,128)})) %all-reduce.8.cloned.1.call-update) | async-done | bytes 1179664 | tf_op jit(solution)/shard_map/psum | solution.py:91
  397.5 11.7 %cholesky.104 = f32[128,128]{1,0:T(8,128)S(1)} custom-call(f32[128,128]{1,0:T(8,128)S(1)} %cholesky.266), custom_call_target="Cholesky" | custom-call | tf_op jit(solution)/shard_map/jit(cholesky)/cholesky | solution.py:93
  409.3 9.8 custom-call.33
  423.5 11.7 %cholesky.217 = f32[128,128]{1,0:T(8,128)S(1)} custom-call(f32[128,128]{1,0:T(8,128)S(1)} %cholesky.270), custom_call_target="Cholesky" | custom-call | tf_op jit(solution)/shard_map/jit(cholesky)/cholesky | solution.py:93
  435.8 10.2 %custom-call.34 = f32[1,128,128]{1,2,0:T(8,128)S(1)} custom-call(f32[1,128,128]{2,1,0:T(8,128)S(1)} %get-tuple-element.61), custom_call_target="InvertDiagBlocksLowerTriangular" | custom-call | tf_op jit(solution)/shard_map/jit(cholesky)/cholesky | solution.py:93
  448.5 11.7 %cholesky.238 = f32[128,128]{1,0:T(8,128)S(1)} custom-call(f32[128,128]{1,0:T(8,128)S(1)} %cholesky.275), custom_call_target="Cholesky" | custom-call | tf_op jit(solution)/shard_map/jit(cholesky)/cholesky | solution.py:93
  461.5 9.8 custom-call.35
  473.6 11.7 %cholesky.255 = f32[128,128]{1,0:T(8,128)S(1)} custom-call(f32[128,128]{1,0:T(8,128)S(1)} %convolution_subtract_fusion.2), custom_call_target="Cholesky" | custom-call | tf_op jit(solution)/shard_map/jit(cholesky)/cholesky | solution.py:93
  492.4 12.0 %while.8 = (s32[]{:T(128)}, f32[512,512]{1,0:T(8,128)}, s32[4,2]{0,1:T(2,128)S(1)}, f32[4,128,128]{2,1,0:T(8,128)S(1)}, s32[]{:T(128)}) while((s32[]{:T(128)}, f32[512,512]{1,0:T(8,128)}, s32[4,2]{0,1:T(2,128)S(1)}, f32[4,128,128]{2,1,0:T(8,128)S(1)}, s32[]{:T(128)}) %tuple.51), condition=%wide.while_cond.1, body=%wide.while_body.1.sunk | while | flops 2 | bytes 131189 | solution.py:97
  504.4 39.3 %custom-call.39 = f32[4,128,128]{1,2,0:T(8,128)S(1)} custom-call(f32[4,128,128]{2,1,0:T(8,128)S(1)} %get-tuple-element.34), custom_call_target="InvertDiagBlocksLowerTriangular" | custom-call | tf_op jit(solution)/shard_map/triangular_solve/custom-call.8 | solution.py:97
  552.5 8.7 all_to_all.49
  561.2 5.4 collective-permute-start.5
  578.6 73.9 %all-reduce.1 = (f32[2,32]{1,0:T(2,128)S(1)}, f32[2,32]{1,0:T(2,128)S(1)}) all-reduce(f32[2,32]{1,0:T(2,128)S(1)} %dynamic_update_slice.22, f32[2,32]{1,0:T(2,128)S(1)} %dynamic_update_slice.21), channel_id=1, replica_groups=mesh['blk'=32,'leaf'=4,'samp'=2] {'blk','leaf','samp'}, use_global_device_ids=true, to_apply=%region_13.17 | all-reduce | flops 128 | bytes 1024 | tf_op jit(solution)/shard_map/psum | solution.py:80
  652.6 161.3 %all-reduce.6.cloned.1.call-done = f32[2,512,32]{1,2,0:T(8,128)} async-done(((f32[2,512,32]{1,2,0:T(8,128)}), f32[2,512,32]{1,2,0:T(8,128)}) %all-reduce.6.cloned.1.call-update) | async-done | bytes 131088 | tf_op jit(solution)/shard_map/psum | solution.py:80
  823.7 75.9 %psum.54 = f32[2,32]{1,0:T(2,128)S(1)} all-reduce(f32[2,32]{1,0:T(2,128)S(1)} %dynamic_update_slice.24), channel_id=1, replica_groups=mesh['blk'=32,'leaf'=4,'samp'=2] {'blk','leaf','samp'}, use_global_device_ids=true, to_apply=%region_16.20 | all-reduce | flops 64 | bytes 512 | tf_op jit(solution)/shard_map/psum | solution.py:80
  899.7 7.2 all_to_all.50
  918.3 74.4 %psum.55 = f32[2,32]{1,0:T(2,128)S(1)} all-reduce(f32[2,32]{1,0:T(2,128)S(1)} %dynamic_update_slice.25), channel_id=1, replica_groups=mesh['blk'=32,'leaf'=4,'samp'=2] {'blk','leaf','samp'}, use_global_device_ids=true, to_apply=%region_18.22 | all-reduce | flops 64 | bytes 512 | tf_op jit(solution)/shard_map/psum | solution.py:80
  (168 shorter events, 118.9 us)
Async XLA Ops:
  40.1 2.1 copy-start
  40.1 10.7 %copy-start.11 = (f32[3,256]{1,0:T(4,128)S(1)}, f32[3,256]{1,0:T(4,128)}, u32[]{:S(2)}) copy-start(f32[3,256]{1,0:T(4,128)} %param.11) | copy-start | bytes 9220
  40.1 14.6 %copy-start.12 = (s32[1,8]{1,0:T(1,128)S(1)}, s32[1,8]{1,0:T(1,128)}, u32[]{:S(2)}) copy-start(s32[1,8]{1,0:T(1,128)} %param.12) | copy-start | bytes 100
  42.2 61.4 %collective-permute-start.1 = (f32[512,1024]{0,1:T(8,128)}, f32[512,1024]{0,1:T(8,128)}, u32[]{:S(2)}, u32[]{:S(2)}) collective-permute-start(f32[512,1024]{0,1:T(8,128)} %bitcast.233), channel_id=1, source_target_pairs={{8,0},{16,8},{24,16},{32,24},{40,32},{48,40},{56,48},{64,56},{72,6... | collective-permute-start | bytes 6291464 | tf_op jit(solution)/shard_map/ppermute | solution.py:17
  50.8 55.8 %collective-permute-start = (f32[512,1024]{0,1:T(8,128)}, f32[512,1024]{0,1:T(8,128)}, u32[]{:S(2)}, u32[]{:S(2)}) collective-permute-start(f32[512,1024]{0,1:T(8,128)} %bitcast.234), channel_id=1, source_target_pairs={{248,0},{0,8},{8,16},{16,24},{24,32},{32,40},{40,48},{48,56},{56,6... | collective-permute-start | bytes 6291464 | tf_op jit(solution)/shard_map/ppermute | solution.py:17
  51.4 7.4 all-to-all-start.1
  54.7 336.6 %all-reduce.8.cloned.1.call-start = ((), (), s32[]{:S(2)}) async-start(), calls=%async_computation.5 | async-start | bytes 2359296 | tf_op jit(solution)/shard_map/psum | solution.py:91
  58.9 35.6 %collective-permute-start.3 = (f32[3,1024]{1,0:T(4,128)S(1)}, f32[3,1024]{1,0:T(4,128)S(1)}, u32[]{:S(2)}, u32[]{:S(2)}) collective-permute-start(f32[3,1024]{1,0:T(4,128)S(1)} %bitcast.253), channel_id=1, source_target_pairs={{8,0},{16,8},{24,16},{32,24},{40,32},{48,40},{56,48},{64,56},{72,6... | collective-permute-start | bytes 36872 | tf_op jit(solution)/shard_map/ppermute | solution.py:17
  64.1 35.7 %collective-permute-start.2 = (f32[3,1024]{1,0:T(4,128)S(1)}, f32[3,1024]{1,0:T(4,128)S(1)}, u32[]{:S(2)}, u32[]{:S(2)}) collective-permute-start(f32[3,1024]{1,0:T(4,128)S(1)} %bitcast.254), channel_id=1, source_target_pairs={{248,0},{0,8},{8,16},{16,24},{24,32},{32,40},{40,48},{48,56},{56,6... | collective-permute-start | bytes 36872 | tf_op jit(solution)/shard_map/ppermute | solution.py:17
  115.4 5.7 copy-start.1
  135.7 3.7 copy-start.5
  135.7 3.7 copy-start.10
  140.0 0.6 copy-start.7
  140.6 673.2 %all-reduce.6.cloned.1.call-start = ((), (), s32[]{:S(2)}) async-start(), calls=%async_computation.4 | async-start | bytes 262144 | tf_op jit(solution)/shard_map/psum | solution.py:80
  396.5 1.0 copy-start.2
  552.5 21.3 %copy-start.3 = (f32[32,256]{1,0:T(8,128)}, f32[32,256]{1,0:T(8,128)S(1)}, u32[]{:S(2)}) copy-start(f32[32,256]{1,0:T(8,128)S(1)} %convolution_subtract_fusion.4) | copy-start | bytes 98308
  561.2 7.3 collective-permute-start.5
  566.6 7.1 collective-permute-start.4
  574.4 78.2 %copy-start.6 = (f32[32,256]{1,0:T(8,128)S(1)}, f32[32,256]{1,0:T(8,128)}, u32[]{:S(2)}) copy-start(f32[32,256]{1,0:T(8,128)} %param.15) | copy-start | bytes 98308
  574.4 239.5 %copy-start.9 = (f32[2,512,32]{1,2,0:T(8,128)S(1)}, f32[2,512,32]{1,2,0:T(8,128)}, u32[]{:S(2)}) copy-start(f32[2,512,32]{1,2,0:T(8,128)} %get-tuple-element.50) | copy-start | bytes 393220
  577.2 322.4 %copy-start.4 = (f32[32,256]{1,0:T(8,128)S(1)}, f32[32,256]{1,0:T(8,128)}, u32[]{:S(2)}) copy-start(f32[32,256]{1,0:T(8,128)} %copy-done.3) | copy-start | bytes 98308
  577.8 0.7 copy-start.8
  907.0 4.1 collective-permute-start.7
  908.5 7.1 collective-permute-start.6
Sparse Core Ops, SparseCore 0:
  140.8 250.4 all-reduce.7
  578.6 235.1 all-reduce.5
